TPU v7x, 256 devices: a whole 4x4x8 slice. The times are simulated.
256 devices in a mesh: pipe: 2 (over core), obs: 16 (over y, x), patch: 8 (over z).
Axes of the slice: x: 4, y: 4, z: 8, core: 2. Of those that a mesh axis runs over, the one named last changes fastest.
Arguments:
- patch_tokens: bfloat16 [4096, 2048], P('patch', 'obs'), may hold values from -40 to 40
- obs_tokens: bfloat16 [2048, 2048], P('patch', 'obs'), may hold values from -40 to 40
- footprint: int32 [32, 8], P('patch'), may hold values from 0 to 15, as said below
- list_counts: int32 [32], P('patch'), may hold values from 1 to 8
- footprint_bias: float32 [32, 8], P('patch'), may hold values from -4 to 290
- w_query: bfloat16 [2, 2048, 2048], P('pipe', None, 'obs'), may hold values from -0.125 to 0.125
- w_key: bfloat16 [2, 2048, 2048], P('pipe', None, 'obs'), may hold values from -0.125 to 0.125
- w_value: bfloat16 [2, 2048, 2048], P('pipe', None, 'obs'), may hold values from -0.125 to 0.125
- w_out: bfloat16 [2, 2048, 2048], P('pipe', 'obs'), may hold values from -0.125 to 0.125
- patch_gain: float32 [2, 2048], P('pipe'), may hold values from 0.1 to 1.9
- obs_gain: float32 [2, 2048], P('pipe'), may hold values from 0.1 to 1.9
Outputs:
- sections: bfloat16 [2, 4096, 2048], P('pipe', 'patch', 'obs')
Inputs may be any that keep to these rules, and one draw needn't show every extreme that they name: `footprint`: entries are global observation block indices. In each row the first list_counts entries (the live ones) are distinct, the rest are to be ignored. For a device along patch and any device along patch, all live entries of the first device's rows that lie in the second device's range of 2 blocks name one and the same block.
All inputs are finite; a program needn't handle non-finite values.
Results may differ from a plain program's by a relative error of at most 0.012.
Values may be sent and summed in bfloat16 or wider, within the bound.
No kernel may reach another device: no remote copies, remote signals or barrier semaphores. Data moves between devices by JAX's collectives and lax.ppermute only.
A program may use at most 64 MiB of HBM per device.

v0:
```python
import jax
import jax.numpy as jnp
from jax import lax
from jax.sharding import PartitionSpec as P

HS = 128
BLK = 128
MB = 128


def passed_along(value, axis, steps):
    count = lax.axis_size(axis)
    first, last = (max(0, -steps), min(count, count - steps))
    return lax.ppermute(value, axis, [(source, source + steps) for source in range(first, last)])


def rms_round(values, gain):
    widened = values.astype(jnp.float32)
    scaled = widened * lax.rsqrt(jnp.mean(widened * widened, axis=-1, keepdims=True) + 1e-05)
    return (scaled * gain).astype(jnp.bfloat16)


def store_rows(sections, out_piece, is_valid, row_start):
    current = lax.dynamic_slice_in_dim(sections, row_start, out_piece.shape[0], 1)
    kept = jnp.where(is_valid, out_piece[None], current)
    return lax.dynamic_update_slice_in_dim(sections, kept, row_start, 1)


def on_device(
    patch_tokens,
    obs_tokens,
    footprint,
    list_counts,
    footprint_bias,
    w_query,
    w_key,
    w_value,
    w_out,
    patch_gain,
    obs_gain,
):
    pipe_segment = lax.axis_index("pipe")
    segment_count = lax.axis_size("pipe")
    obs_column = lax.axis_index("obs")
    feature_part = patch_tokens.shape[1]
    full_features = feature_part * lax.axis_size("obs")
    head_width = w_query.shape[2]
    heads_here = head_width // HS
    list_slots = footprint.shape[1]
    micro_count = patch_tokens.shape[0] // MB
    blocks_micro = MB // BLK
    score_scale = HS ** (-0.5)
    observed = lax.all_gather(obs_tokens, "obs", axis=1, tiled=True)
    obs_normed = rms_round(observed, obs_gain[0])
    key_values = jnp.concatenate(
        [
            jnp.dot(obs_normed, w_key[0], preferred_element_type=jnp.float32).astype(jnp.bfloat16),
            jnp.dot(obs_normed, w_value[0], preferred_element_type=jnp.float32).astype(
                jnp.bfloat16
            ),
        ],
        axis=1,
    )
    local_blocks = key_values.reshape(-1, BLK, 2 * head_width)
    kv_table = lax.all_gather(local_blocks, "patch", axis=0, tiled=True)

    def attend_block(segment_input, micro_index):
        patch_normed = rms_round(segment_input, patch_gain[0])
        queries = (
            jnp.dot(patch_normed, w_query[0], preferred_element_type=jnp.float32) * score_scale
        ).astype(jnp.bfloat16)
        queries = queries.reshape(blocks_micro, BLK, heads_here, HS)
        first_block = micro_index * blocks_micro
        slot_part = lax.dynamic_slice_in_dim(footprint, first_block, blocks_micro, 0)
        count_part = lax.dynamic_slice_in_dim(list_counts, first_block, blocks_micro, 0)
        bias_part = lax.dynamic_slice_in_dim(footprint_bias, first_block, blocks_micro, 0)
        picked = kv_table[slot_part].reshape(blocks_micro, list_slots * BLK, 2 * head_width)
        key_part = picked[:, :, :head_width].reshape(blocks_micro, list_slots * BLK, heads_here, HS)
        value_part = picked[:, :, head_width:].reshape(
            blocks_micro, list_slots * BLK, heads_here, HS
        )
        scores = jnp.einsum(
            "bqhd,bkhd->bhqk", queries, key_part, preferred_element_type=jnp.float32
        )
        alive_mask = jnp.repeat(jnp.arange(list_slots)[None, :] < count_part[:, None], BLK, axis=1)
        added = jnp.repeat(bias_part, BLK, axis=1)
        scores = jnp.where(alive_mask[:, None, None, :], scores + added[:, None, None, :], -1e30)
        row_max = jnp.max(scores, axis=-1, keepdims=True)
        weights = jnp.exp(scores - row_max)
        weights = (weights / jnp.sum(weights, axis=-1, keepdims=True)).astype(jnp.bfloat16)
        context = jnp.einsum(
            "bhqk,bkhd->bqhd", weights, value_part, preferred_element_type=jnp.float32
        ).astype(jnp.bfloat16)
        context = context.reshape(MB, head_width)
        return jnp.dot(context, w_out[0], preferred_element_type=jnp.float32)

    def spare_block(segment_input, micro_index):
        return jnp.zeros((MB, full_features), jnp.float32)

    tick_total = micro_count + segment_count - 1
    sections = jnp.zeros((1, patch_tokens.shape[0], feature_part), jnp.bfloat16)
    rows_all = lax.all_gather(patch_tokens, "obs", axis=1, tiled=True)
    arriving = jnp.zeros((MB, full_features), jnp.bfloat16)
    for tick_num in range(tick_total):
        tick_micro = tick_num - pipe_segment
        is_valid = (tick_micro >= 0) & (tick_micro < micro_count)
        micro_index = jnp.clip(tick_micro, 0, micro_count - 1)
        own_rows = lax.dynamic_slice_in_dim(rows_all, micro_index * MB, MB, 0)
        segment_input = jnp.where(pipe_segment == 0, own_rows, arriving)
        partial_value = lax.cond(is_valid, attend_block, spare_block, segment_input, micro_index)
        head_total = lax.psum(partial_value.astype(jnp.bfloat16), "obs").astype(jnp.float32)
        segment_output = (segment_input.astype(jnp.float32) + head_total).astype(jnp.bfloat16)
        out_piece = lax.dynamic_slice_in_dim(
            segment_output, obs_column * feature_part, feature_part, 1
        )
        sections = store_rows(sections, out_piece, is_valid, micro_index * MB)
        if tick_num + 1 < tick_total:
            arriving = passed_along(segment_output, "pipe", 1)
    return sections


def solution(mesh):
    in_specs = (
        P("patch", "obs"),
        P("patch", "obs"),
        P("patch", None),
        P("patch"),
        P("patch", None),
        P("pipe", None, "obs"),
        P("pipe", None, "obs"),
        P("pipe", None, "obs"),
        P("pipe", "obs", None),
        P("pipe", None),
        P("pipe", None),
    )
    out_specs = P("pipe", "patch", "obs")
    return jax.shard_map(
        on_device, mesh=mesh, in_specs=in_specs, out_specs=out_specs, check_vma=False
    )
```

profile of v0, /device:TPU:2, one launch (start us, length us, event | category | flops | bytes accessed | tf_op | source)
XLA Modules:
  0.0 700.2 jit_solution(2485516238832570236)
XLA Ops:
  8.1 52.5 %all-gather.6.cloned.1.call-done = bf16[256,2048]{1,0:T(8,128)(2,1)} async-done(((bf16[256,128]{1,0:T(8,128)(2,1)}), bf16[256,2048]{1,0:T(8,128)(2,1)}) %all-gather.6.cloned.1.call-update) | async-done | bytes 1048592 | tf_op jit(solution)/shard_map/all_gather | solution.py:53
  60.6 1.6 fusion.120
  62.2 1.8 convolution_convert_fusion.5
  65.5 48.9 %all-gather.4.cloned.1.call-done = bf16[512,2048]{1,0:T(8,128)(2,1)} async-done(((bf16[512,128]{1,0:T(8,128)(2,1)}), bf16[512,2048]{1,0:T(8,128)(2,1)}) %all-gather.4.cloned.1.call-update) | async-done | bytes 2097168 | tf_op jit(solution)/shard_map/all_gather | solution.py:102
  114.4 1.1 dynamic-slice_select_fusion.4
  115.6 38.8 %all-gather.8.cloned.1.call-done = bf16[16,128,256]{2,1,0:T(8,128)(2,1)} async-done(((bf16[2,128,256]{2,1,0:T(8,128)(2,1)}), bf16[16,128,256]{2,1,0:T(8,128)(2,1)}) %all-gather.8.cloned.1.call-update) | async-done | bytes 1048592 | tf_op jit(solution)/shard_map/all_gather | solution.py:65
  154.4 6.1 conditional.5
  154.5 1.8 gather_fusion
  158.7 1.8 fusion.3
  161.4 93.9 %all-reduce.6.cloned.1.call-done = bf16[128,2048]{1,0:T(8,128)(2,1)} async-done(((bf16[128,2048]{1,0:T(8,128)(2,1)}), bf16[128,2048]{1,0:T(8,128)(2,1)}) %all-reduce.6.cloned.1.call-update) | async-done | bytes 524304 | tf_op jit(solution)/shard_map/psum | solution.py:111
  255.3 2.1 add_convert_fusion.3
  257.5 1.3 collective-permute-start
  258.8 1.7 collective-permute-done
  260.5 1.2 dynamic-slice_select_fusion.3
  261.7 6.7 conditional.6
  264.6 1.6 fusion.138
  266.5 1.9 fusion.27
  268.4 0.8 copy-done.3
  269.3 95.4 %all-reduce.8.cloned.1.call-done = bf16[128,2048]{1,0:T(8,128)(2,1)} async-done(((bf16[128,2048]{1,0:T(8,128)(2,1)}), bf16[128,2048]{1,0:T(8,128)(2,1)}) %all-reduce.8.cloned.1.call-update) | async-done | bytes 524304 | tf_op jit(solution)/shard_map/psum | solution.py:111
  364.6 1.2 add_convert_fusion.2
  365.8 1.3 collective-permute-start.1
  367.1 1.5 collective-permute-done.1
  368.6 1.2 dynamic-slice_select_fusion.2
  369.8 7.7 %conditional.7 = (bf16[128,2048]{1,0:T(8,128)(2,1)S(1)}) conditional(s32[]{:T(128)} %convert_element_type.212, () %tuple.39, (s32[]{:T(128)}, s32[4,8]{1,0:T(4,128)S(1)}, bf16[16,128,256]{2,1,0:T(8,128)(2,1)S(1)}, s32[4]{0:T(128)S(1)}, bf16[128,2048]{1,0:T(8,128)(2,1)S(1)}, /*index=5*/f32[1,2048]{1,0:T(1,128)S(1)}, ...), branch_computations={%region_13.14_spmd, %region_14.18_spmd} | conditional | flops 204260256 | bytes 7891790 | solution.py:110
  369.9 1.4 gather_fusion.2
  372.7 1.7 fusion.143
  374.4 0.8 copy-done.10
  375.4 2.0 fusion.51
  377.5 0.8 copy-done.4
  378.4 95.4 %all-reduce.10.cloned.1.call-done = bf16[128,2048]{1,0:T(8,128)(2,1)} async-done(((bf16[128,2048]{1,0:T(8,128)(2,1)}), bf16[128,2048]{1,0:T(8,128)(2,1)}) %all-reduce.10.cloned.1.call-update) | async-done | bytes 524304 | tf_op jit(solution)/shard_map/psum | solution.py:111
  473.7 1.2 add_convert_fusion.1
  474.9 2.1 collective-permute-start.2
  477.0 0.8 collective-permute-done.2
  477.9 1.2 dynamic-slice_select_fusion.1
  479.1 7.8 %conditional.8 = (bf16[128,2048]{1,0:T(8,128)(2,1)S(1)}) conditional(s32[]{:T(128)} %convert_element_type.217, () %tuple.41, (s32[]{:T(128)}, s32[4,8]{1,0:T(4,128)S(1)}, bf16[16,128,256]{2,1,0:T(8,128)(2,1)S(1)}, s32[4]{0:T(128)S(1)}, bf16[128,2048]{1,0:T(8,128)(2,1)S(1)}, /*index=5*/f32[1,2048]{1,0:T(1,128)S(1)}, ...), branch_computations={%region_19.20_spmd, %region_20.24_spmd} | conditional | flops 204260256 | bytes 7891790 | solution.py:110
  479.2 1.4 gather_fusion.3
  482.1 1.7 fusion.148
  483.9 0.8 copy-done.11
  484.9 2.0 fusion.75
  486.9 0.8 copy-done.5
  487.8 95.6 %all-reduce.12.cloned.1.call-done = bf16[128,2048]{1,0:T(8,128)(2,1)} async-done(((bf16[128,2048]{1,0:T(8,128)(2,1)}), bf16[128,2048]{1,0:T(8,128)(2,1)}) %all-reduce.12.cloned.1.call-update) | async-done | bytes 524304 | tf_op jit(solution)/shard_map/psum | solution.py:111
  583.3 1.2 add_convert_fusion
  584.5 2.1 collective-permute-start.3
  586.6 0.8 collective-permute-done.3
  587.5 1.2 dynamic-slice_select_fusion
  590.4 0.8 fusion.131
  591.2 100.7 %all-reduce.14.cloned.1.call-done = bf16[128,2048]{1,0:T(8,128)(2,1)} async-done(((bf16[128,2048]{1,0:T(8,128)(2,1)}), bf16[128,2048]{1,0:T(8,128)(2,1)}) %all-reduce.14.cloned.1.call-update) | async-done | bytes 524304 | tf_op jit(solution)/shard_map/psum | solution.py:111
  691.9 1.4 fusion.129
  (105 shorter events, 15.0 us)
Async XLA Ops:
  6.5 55.6 %copy-start = (bf16[1,2048,128]{2,1,0:T(8,128)(2,1)S(1)}, bf16[1,2048,128]{2,1,0:T(8,128)(2,1)}, u32[]{:S(2)}) copy-start(bf16[1,2048,128]{2,1,0:T(8,128)(2,1)} %param.28) | copy-start | bytes 1572868
  6.5 57.4 %copy-start.16 = (f32[1,2048]{1,0:T(1,128)S(1)}, f32[1,2048]{1,0:T(1,128)}, u32[]{:S(2)}) copy-start(f32[1,2048]{1,0:T(1,128)} %param.31) | copy-start | bytes 24580
  6.5 57.4 %copy-start.13 = (bf16[1,2048,128]{2,1,0:T(8,128)(2,1)S(1)}, bf16[1,2048,128]{2,1,0:T(8,128)(2,1)}, u32[]{:S(2)}) copy-start(bf16[1,2048,128]{2,1,0:T(8,128)(2,1)} %param.27) | copy-start | bytes 1572868
  6.5 54.0 %all-gather.6.cloned.1.call-start = ((), (), s32[]{:S(2)}) async-start(), calls=%async_computation.1 | async-start | bytes 1114112 | tf_op jit(solution)/shard_map/all_gather | solution.py:53
  7.3 107.2 %all-gather.4.cloned.1.call-start = ((), (), s32[]{:S(2)}) async-start(), calls=%async_computation | async-start | bytes 2228224 | tf_op jit(solution)/shard_map/all_gather | solution.py:102
  8.0 146.4 %all-gather.8.cloned.1.call-start = ((), (), s32[]{:S(2)}) async-start(), calls=%async_computation.2 | async-start | bytes 1179648 | tf_op jit(solution)/shard_map/all_gather | solution.py:65
  60.5 3.4 copy-start.7
  64.0 90.4 %copy-start.14 = (bf16[1,2048,128]{2,1,0:T(8,128)(2,1)S(1)}, bf16[1,2048,128]{2,1,0:T(8,128)(2,1)}, u32[]{:S(2)}) copy-start(bf16[1,2048,128]{2,1,0:T(8,128)(2,1)} %param.26) | copy-start | bytes 1572868
  64.0 90.4 %copy-start.17 = (f32[1,2048]{1,0:T(1,128)S(1)}, f32[1,2048]{1,0:T(1,128)}, u32[]{:S(2)}) copy-start(f32[1,2048]{1,0:T(1,128)} %param.30) | copy-start | bytes 24580
  64.0 90.4 %copy-start.18 = (s32[4,8]{1,0:T(4,128)S(1)}, s32[4,8]{1,0:T(4,128)}, u32[]{:S(2)}) copy-start(s32[4,8]{1,0:T(4,128)} %param.23) | copy-start | bytes 388
  64.0 90.4 %copy-start.19 = (f32[4,8]{1,0:T(4,128)S(1)}, f32[4,8]{1,0:T(4,128)}, u32[]{:S(2)}) copy-start(f32[4,8]{1,0:T(4,128)} %param.25) | copy-start | bytes 388
  64.0 90.3 %copy-start.20 = (s32[4]{0:T(128)S(1)}, s32[4]{0:T(128)}, u32[]{:S(2)}) copy-start(s32[4]{0:T(128)} %param.24) | copy-start | bytes 52
  65.4 189.9 %all-reduce.6.cloned.1.call-start = ((), (), s32[]{:S(2)}) async-start(), calls=%async_computation.3 | async-start | bytes 1048576 | tf_op jit(solution)/shard_map/psum | solution.py:111
  160.5 0.8 copy-start.2
  160.5 101.1 %copy-start.1 = (bf16[16,128,256]{2,1,0:T(8,128)(2,1)S(1)}, bf16[16,128,256]{2,1,0:T(8,128)(2,1)}, u32[]{:S(2)}) copy-start(bf16[16,128,256]{2,1,0:T(8,128)(2,1)} %all-gather.8.cloned.1.call-done) | copy-start | bytes 3145732
  161.3 203.3 %all-reduce.8.cloned.1.call-start = ((), (), s32[]{:S(2)}) async-start(), calls=%async_computation.4 | async-start | bytes 1048576 | tf_op jit(solution)/shard_map/psum | solution.py:111
  257.5 3.0 collective-permute-start
  261.7 0.8 copy-start.15
  263.1 3.1 copy-start.12
  268.4 0.8 copy-start.3
  269.2 204.5 %all-reduce.10.cloned.1.call-start = ((), (), s32[]{:S(2)}) async-start(), calls=%async_computation.5 | async-start | bytes 1048576 | tf_op jit(solution)/shard_map/psum | solution.py:111
  365.8 2.8 collective-permute-start.1
  374.4 0.8 copy-start.10
  377.5 0.8 copy-start.4
  378.3 205.0 %all-reduce.12.cloned.1.call-start = ((), (), s32[]{:S(2)}) async-start(), calls=%async_computation.6 | async-start | bytes 1048576 | tf_op jit(solution)/shard_map/psum | solution.py:111
  474.9 4.1 copy-start.8
  474.9 2.9 collective-permute-start.2
  483.8 0.8 copy-start.11
  486.9 0.8 copy-start.5
  487.7 204.2 %all-reduce.14.cloned.1.call-start = ((), (), s32[]{:S(2)}) async-start(), calls=%async_computation.7 | async-start | bytes 1048576 | tf_op jit(solution)/shard_map/psum | solution.py:111
  584.5 2.9 collective-permute-start.3
  588.7 0.8 copy-start.6
  591.2 100.7 %copy-start.9 = (bf16[1,512,128]{2,1,0:T(8,128)(2,1)}, bf16[1,512,128]{2,1,0:T(8,128)(2,1)S(1)}, u32[]{:S(2)}) copy-start(bf16[1,512,128]{2,1,0:T(8,128)(2,1)S(1)} %fusion.130) | copy-start | bytes 393220
Sparse Core Ops, SparseCore 0:
  9.7 50.7 all-gather.5
  63.0 51.4 all-gather.3
  116.2 38.1 all-gather.7
  161.4 93.8 all-reduce.5
  269.3 95.2 all-reduce.7
  378.4 95.2 all-reduce.9
  487.9 95.4 all-reduce.11
  589.6 102.2 all-reduce.13
where the time goes:
time: 701 us; the launch traced here: 700 us
  waiting for transfers between devices  628 us (90%)
  other arithmetic  20.3 us (3%)
  matrix products  15.8 us (2%)
  local copies, waits for them, and re-layouts  15.4 us (2%)
  between operations  13.8 us (2%)
  starting transfers between devices  7.12 us (1%)
    psum x5, waiting for transfers between devices, on_device(): lax.psum(partial_value.astype(jnp.bfloat16), 'obs').astype(jnp.float32)  481 us
    all_gather x1, waiting for transfers between devices, on_device(): observed = lax.all_gather(obs_tokens, 'obs', axis=1, tiled=True)  52.5 us
    all_gather x1, waiting for transfers between devices, on_device(): rows_all = lax.all_gather(patch_tokens, 'obs', axis=1, tiled=True)  48.9 us
    all_gather x1, waiting for transfers between devices, on_device(): kv_table = lax.all_gather(local_blocks, 'patch', axis=0, tiled=True)  38.8 us
  transfers between devices with their start and end apart: 12, of which 12 were waited for; matrix products, arithmetic and copies ran while one was open for 1% of the time, Pallas kernels for 0%

commit v1 on v0

--- a/solution.py
+++ b/solution.py
@@ -1,3 +1,4 @@
+import functools
 import jax
 import jax.numpy as jnp
 from jax import lax
@@ -6,6 +7,18 @@
 HS = 128
 BLK = 128
 MB = 128
+
+
+def entries_feed(field_in, axis_k):
+    return jnp.concatenate(
+        jax.lax.all_to_all(
+            jnp.stack([field_in for _ in range(jax.lax.axis_size("patch"))], 0), "patch", 0, 0
+        ),
+        axis_k,
+    )
+
+
+core_hold = functools.partial(entries_feed, axis_k=0)
 
 
 def passed_along(value, axis, steps):
@@ -62,7 +75,7 @@
         axis=1,
     )
     local_blocks = key_values.reshape(-1, BLK, 2 * head_width)
-    kv_table = lax.all_gather(local_blocks, "patch", axis=0, tiled=True)
+    kv_table = core_hold(local_blocks)
 
     def attend_block(segment_input, micro_index):
         patch_normed = rms_round(segment_input, patch_gain[0])

time: 701 us -> 662 us (0.944)
  waiting for transfers between devices: 628 us -> 582 us
    all_gather x1 -> x0, waiting for transfers between devices: 38.8 us -> none  [on_device(): kv_table = lax.all_gather(local_blocks, 'patch', axis=0, tiled=True)]
    all_gather x1, waiting for transfers between devices: 48.9 us -> 41.5 us  [on_device(): rows_all = lax.all_gather(patch_tokens, 'obs', axis=1, tiled=True)]
    all_to_all x0 -> x1, starting transfers between devices: none -> 7.02 us  [entries_feed(): jax.lax.all_to_all(jnp.stack([field_in for _ in range(jax.lax.axis_size('...]
  transfers between devices with their start and end apart: 12 -> 12, of which waited for: 12 -> 11; matrix products, arithmetic and copies ran while one was open for 1% -> 1% of each run, Pallas kernels for 0% -> 0%
where the time goes in v1:
time: 662 us; the launch traced here: 661 us
  waiting for transfers between devices  582 us (88%)
  other arithmetic  20.2 us (3%)
  matrix products  16.8 us (3%)
  starting transfers between devices  14.1 us (2%)
  between operations  13.8 us (2%)
  local copies, waits for them, and re-layouts  13.7 us (2%)
    psum x5, waiting for transfers between devices, on_device(): lax.psum(partial_value.astype(jnp.bfloat16), 'obs').astype(jnp.float32)  482 us
    all_gather x1, waiting for transfers between devices, on_device(): observed = lax.all_gather(obs_tokens, 'obs', axis=1, tiled=True)  52.5 us
    all_gather x1, waiting for transfers between devices, on_device(): rows_all = lax.all_gather(patch_tokens, 'obs', axis=1, tiled=True)  41.5 us
  transfers between devices with their start and end apart: 12, of which 11 were waited for; matrix products, arithmetic and copies ran while one was open for 1% of the time, Pallas kernels for 0%

profile of v1, /device:TPU:2, one launch (start us, length us, event | category | flops | bytes accessed | tf_op | source)
XLA Modules:
  0.0 661.2 jit_solution(1966888730843323600)
XLA Ops:
  8.0 52.5 %all-gather.5.cloned.1.call-done = bf16[256,2048]{1,0:T(8,128)(2,1)} async-done(((bf16[256,128]{1,0:T(8,128)(2,1)}), bf16[256,2048]{1,0:T(8,128)(2,1)}) %all-gather.5.cloned.1.call-update) | async-done | bytes 1048592 | tf_op jit(solution)/shard_map/all_gather | solution.py:66
  60.6 1.6 fusion.120
  62.2 1.8 convolution_convert_fusion.5
  64.7 1.1 stack.3
  65.8 7.0 %all-to-all-start = ((bf16[8,2,128,256]{3,2,1,0:T(8,128)(2,1)}), bf16[8,2,128,256]{3,2,1,0:T(8,128)(2,1)S(1)}, u32[]{:S(2)}, u32[]{:S(2)}) async-start(bf16[8,2,128,256]{3,2,1,0:T(8,128)(2,1)} %stack.3), calls=%async_computation | async-start | bytes 2097152 | tf_op jit(solution)/shard_map/all_to_all | solution.py:14
  72.9 41.5 %all-gather.3.cloned.1.call-done = bf16[512,2048]{1,0:T(8,128)(2,1)} async-done(((bf16[512,128]{1,0:T(8,128)(2,1)}), bf16[512,2048]{1,0:T(8,128)(2,1)}) %all-gather.3.cloned.1.call-update) | async-done | bytes 2097168 | tf_op jit(solution)/shard_map/all_gather | solution.py:115
  114.4 1.1 dynamic-slice_select_fusion.4
  115.6 5.9 conditional.5
  117.8 1.6 fusion.133
  119.7 1.8 fusion.3
  121.5 0.8 copy-done.1
  122.4 95.2 %all-reduce.6.cloned.1.call-done = bf16[128,2048]{1,0:T(8,128)(2,1)} async-done(((bf16[128,2048]{1,0:T(8,128)(2,1)}), bf16[128,2048]{1,0:T(8,128)(2,1)}) %all-reduce.6.cloned.1.call-update) | async-done | bytes 524304 | tf_op jit(solution)/shard_map/psum | solution.py:124
  217.6 2.2 add_convert_fusion.3
  219.8 1.3 collective-permute-start
  221.1 1.7 collective-permute-done
  222.8 1.2 dynamic-slice_select_fusion.3
  224.0 6.0 conditional.6
  226.2 1.6 fusion.138
  228.0 1.9 fusion.27
  230.8 95.3 %all-reduce.8.cloned.1.call-done = bf16[128,2048]{1,0:T(8,128)(2,1)} async-done(((bf16[128,2048]{1,0:T(8,128)(2,1)}), bf16[128,2048]{1,0:T(8,128)(2,1)}) %all-reduce.8.cloned.1.call-update) | async-done | bytes 524304 | tf_op jit(solution)/shard_map/psum | solution.py:124
  326.1 1.2 add_convert_fusion.2
  327.3 1.3 collective-permute-start.1
  328.6 1.5 collective-permute-done.1
  330.1 1.2 dynamic-slice_select_fusion.2
  331.3 7.7 %conditional.7 = (bf16[128,2048]{1,0:T(8,128)(2,1)S(1)}) conditional(s32[]{:T(128)} %convert_element_type.212, () %tuple.39, (s32[]{:T(128)}, s32[4,8]{1,0:T(4,128)S(1)}, bf16[16,128,256]{2,1,0:T(8,128)(2,1)S(1)}, s32[4]{0:T(128)S(1)}, bf16[128,2048]{1,0:T(8,128)(2,1)S(1)}, /*index=5*/f32[1,2048]{1,0:T(1,128)S(1)}, ...), branch_computations={%region_13.14_spmd, %region_14.18_spmd} | conditional | flops 204260256 | bytes 7891790 | solution.py:123
  331.4 1.4 gather_fusion.2
  334.1 1.7 fusion.143
  336.9 2.0 fusion.51
  339.8 95.3 %all-reduce.10.cloned.1.call-done = bf16[128,2048]{1,0:T(8,128)(2,1)} async-done(((bf16[128,2048]{1,0:T(8,128)(2,1)}), bf16[128,2048]{1,0:T(8,128)(2,1)}) %all-reduce.10.cloned.1.call-update) | async-done | bytes 524304 | tf_op jit(solution)/shard_map/psum | solution.py:124
  435.1 1.2 add_convert_fusion.1
  436.3 2.1 collective-permute-start.2
  438.4 0.9 collective-permute-done.2
  439.2 1.2 dynamic-slice_select_fusion.1
  440.4 7.7 %conditional.8 = (bf16[128,2048]{1,0:T(8,128)(2,1)S(1)}) conditional(s32[]{:T(128)} %convert_element_type.217, () %tuple.41, (s32[]{:T(128)}, s32[4,8]{1,0:T(4,128)S(1)}, bf16[16,128,256]{2,1,0:T(8,128)(2,1)S(1)}, s32[4]{0:T(128)S(1)}, bf16[128,2048]{1,0:T(8,128)(2,1)S(1)}, /*index=5*/f32[1,2048]{1,0:T(1,128)S(1)}, ...), branch_computations={%region_19.20_spmd, %region_20.24_spmd} | conditional | flops 204260256 | bytes 7891790 | solution.py:123
  440.5 1.4 gather_fusion.3
  443.3 1.7 fusion.148
  445.0 0.8 copy-done.10
  446.1 2.0 fusion.75
  448.1 0.8 copy-done.4
  449.0 95.5 %all-reduce.12.cloned.1.call-done = bf16[128,2048]{1,0:T(8,128)(2,1)} async-done(((bf16[128,2048]{1,0:T(8,128)(2,1)}), bf16[128,2048]{1,0:T(8,128)(2,1)}) %all-reduce.12.cloned.1.call-update) | async-done | bytes 524304 | tf_op jit(solution)/shard_map/psum | solution.py:124
  544.5 1.2 add_convert_fusion
  545.7 2.1 collective-permute-start.3
  547.8 0.9 collective-permute-done.3
  548.6 1.2 dynamic-slice_select_fusion
  549.9 0.8 copy-done.5
  551.6 0.8 fusion.131
  552.4 100.5 %all-reduce.14.cloned.1.call-done = bf16[128,2048]{1,0:T(8,128)(2,1)} async-done(((bf16[128,2048]{1,0:T(8,128)(2,1)}), bf16[128,2048]{1,0:T(8,128)(2,1)}) %all-reduce.14.cloned.1.call-update) | async-done | bytes 524304 | tf_op jit(solution)/shard_map/psum | solution.py:124
  652.9 1.4 fusion.129
  (99 shorter events, 14.0 us)
Async XLA Ops:
  6.5 55.6 %copy-start = (bf16[1,2048,128]{2,1,0:T(8,128)(2,1)S(1)}, bf16[1,2048,128]{2,1,0:T(8,128)(2,1)}, u32[]{:S(2)}) copy-start(bf16[1,2048,128]{2,1,0:T(8,128)(2,1)} %param.28) | copy-start | bytes 1572868
  6.5 57.4 %copy-start.13 = (f32[1,2048]{1,0:T(1,128)S(1)}, f32[1,2048]{1,0:T(1,128)}, u32[]{:S(2)}) copy-start(f32[1,2048]{1,0:T(1,128)} %param.31) | copy-start | bytes 24580
  6.5 57.4 %copy-start.12 = (bf16[1,2048,128]{2,1,0:T(8,128)(2,1)S(1)}, bf16[1,2048,128]{2,1,0:T(8,128)(2,1)}, u32[]{:S(2)}) copy-start(bf16[1,2048,128]{2,1,0:T(8,128)(2,1)} %param.27) | copy-start | bytes 1572868
  6.5 54.0 %all-gather.5.cloned.1.call-start = ((), (), s32[]{:S(2)}) async-start(), calls=%async_computation.2 | async-start | bytes 1114112 | tf_op jit(solution)/shard_map/all_gather | solution.py:66
  7.3 107.2 %all-gather.3.cloned.1.call-start = ((), (), s32[]{:S(2)}) async-start(), calls=%async_computation.1 | async-start | bytes 2228224 | tf_op jit(solution)/shard_map/all_gather | solution.py:115
  60.5 3.4 copy-start.6
  64.7 50.9 %copy-start.14 = (f32[1,2048]{1,0:T(1,128)S(1)}, f32[1,2048]{1,0:T(1,128)}, u32[]{:S(2)}) copy-start(f32[1,2048]{1,0:T(1,128)} %param.30) | copy-start | bytes 24580
  64.7 50.9 %copy-start.15 = (s32[4,8]{1,0:T(4,128)S(1)}, s32[4,8]{1,0:T(4,128)}, u32[]{:S(2)}) copy-start(s32[4,8]{1,0:T(4,128)} %param.23) | copy-start | bytes 388
  64.7 50.9 %copy-start.16 = (f32[4,8]{1,0:T(4,128)S(1)}, f32[4,8]{1,0:T(4,128)}, u32[]{:S(2)}) copy-start(f32[4,8]{1,0:T(4,128)} %param.25) | copy-start | bytes 388
  64.7 50.9 %copy-start.17 = (s32[4]{0:T(128)S(1)}, s32[4]{0:T(128)}, u32[]{:S(2)}) copy-start(s32[4]{0:T(128)} %param.24) | copy-start | bytes 52
  65.8 49.7 %all-to-all-start = ((bf16[8,2,128,256]{3,2,1,0:T(8,128)(2,1)}), bf16[8,2,128,256]{3,2,1,0:T(8,128)(2,1)S(1)}, u32[]{:S(2)}, u32[]{:S(2)}) async-start(bf16[8,2,128,256]{3,2,1,0:T(8,128)(2,1)} %stack.3), calls=%async_computation | async-start | bytes 2097152 | tf_op jit(solution)/shard_map/all_to_all | solution.py:14
  72.9 144.8 %all-reduce.6.cloned.1.call-start = ((), (), s32[]{:S(2)}) async-start(), calls=%async_computation.3 | async-start | bytes 1048576 | tf_op jit(solution)/shard_map/psum | solution.py:124
  121.5 0.8 copy-start.1
  122.3 203.8 %all-reduce.8.cloned.1.call-start = ((), (), s32[]{:S(2)}) async-start(), calls=%async_computation.4 | async-start | bytes 1048576 | tf_op jit(solution)/shard_map/psum | solution.py:124
  219.8 3.0 collective-permute-start
  224.7 3.2 copy-start.11
  229.9 0.8 copy-start.2
  230.7 204.3 %all-reduce.10.cloned.1.call-start = ((), (), s32[]{:S(2)}) async-start(), calls=%async_computation.5 | async-start | bytes 1048576 | tf_op jit(solution)/shard_map/psum | solution.py:124
  327.3 2.8 collective-permute-start.1
  335.8 0.8 copy-start.9
  338.9 0.8 copy-start.3
  339.7 204.8 %all-reduce.12.cloned.1.call-start = ((), (), s32[]{:S(2)}) async-start(), calls=%async_computation.6 | async-start | bytes 1048576 | tf_op jit(solution)/shard_map/psum | solution.py:124
  436.3 4.1 copy-start.7
  436.3 2.9 collective-permute-start.2
  445.0 0.8 copy-start.10
  448.1 0.8 copy-start.4
  448.9 204.0 %all-reduce.14.cloned.1.call-start = ((), (), s32[]{:S(2)}) async-start(), calls=%async_computation.7 | async-start | bytes 1048576 | tf_op jit(solution)/shard_map/psum | solution.py:124
  545.7 2.9 collective-permute-start.3
  549.9 0.8 copy-start.5
  552.4 100.5 %copy-start.8 = (bf16[1,512,128]{2,1,0:T(8,128)(2,1)}, bf16[1,512,128]{2,1,0:T(8,128)(2,1)S(1)}, u32[]{:S(2)}) copy-start(bf16[1,512,128]{2,1,0:T(8,128)(2,1)S(1)} %fusion.130) | copy-start | bytes 393220
Sparse Core Ops, SparseCore 0:
  9.7 50.7 all-gather.4
  63.0 51.4 all-gather.2
  122.4 95.1 all-reduce.5
  230.9 95.1 all-reduce.7
  339.8 95.1 all-reduce.9
  449.1 95.4 all-reduce.11
  550.8 102.0 all-reduce.13
